TPU v7x, 32 devices: a whole 2x2x4 slice. The times are simulated.
32 devices in a mesh: req: 8 (over z, x), tp: 4 (over y, core).
Axes of the slice: x: 2, y: 2, z: 4, core: 2. Of those that a mesh axis runs over, the one named last changes fastest.
Arguments:
- tokens: bfloat16 [4096, 3584], P('req'), may hold values from -400 to 400, as said below
- norm_gain: float32 [3584], P(('req', 'tp')), may hold values from 0.5 to 1.5
- qkv_weight: float32 [3584, 4608], P(('req', 'tp')), may hold values from -0.09375 to 0.09375
- qkv_bias: float32 [4608], P(('req', 'tp')), may hold values from -48 to 48
- lengths: int32 [8, 4], P('req'), may hold values from 1 to 256, 512 in all within a row
Outputs:
- context: bfloat16 [4096, 3584], P('req', 'tp')
Inputs may be any that keep to these rules, and one draw needn't show every extreme that they name: `tokens`: hidden states of order one to some hundreds. Each replica's tenant lengths sum to 512, the largest is exactly 256.
All inputs are finite; a program needn't handle non-finite values.
Results may differ from a plain program's by a relative error of at most 0.009.
The roundings to bfloat16 on the way count: a program that leaves them out, or rounds other values in their place, can miss the bound.
Values may be sent and summed in bfloat16 or wider, within the bound.
A program may use at most 128 MiB of HBM per device.

v0:
```python
import math
import jax
import jax.numpy as jnp
from jax import lax
from jax.sharding import PartitionSpec as P

HEAD_DIM = 128
SINKS = 4
GROUP = 7
WINDOW = 160


def normalize(values, gain):
    wide = values.astype(jnp.float32)
    meansq = jnp.mean(wide * wide, axis=-1, keepdims=True)
    return (wide * lax.rsqrt(meansq + 1e-06) * gain.astype(jnp.float32)).astype(jnp.bfloat16)


def positions(lens, count):
    index = jnp.arange(count, dtype=jnp.int32)
    ends = jnp.cumsum(lens)
    after = index[:, None] >= ends[None, :]
    tenant = jnp.sum(after.astype(jnp.int32), axis=1)
    start = jnp.sum(jnp.where(after, lens[None, :], 0), axis=1)
    return (tenant, index - start)


def rotate(values, pos):
    half = HEAD_DIM // 2
    freqs = jnp.exp(-(jnp.arange(half, dtype=jnp.float32) * 2.0 / HEAD_DIM) * math.log(1000000.0))
    angle = pos.astype(jnp.float32)[:, None] * freqs[None, :]
    cosine = jnp.concatenate([jnp.cos(angle), jnp.cos(angle)], axis=-1)
    sine = jnp.concatenate([jnp.sin(angle), jnp.sin(angle)], axis=-1)
    shape = (values.shape[0],) + (1,) * (values.ndim - 2) + (HEAD_DIM,)
    cosine = cosine.reshape(shape)
    sine = sine.reshape(shape)
    turned = jnp.concatenate([-values[..., half:], values[..., :half]], axis=-1)
    return values * cosine + turned * sine


def attend(joined, tenant, pos):
    count = joined.shape[0]
    blocks = joined.reshape(count, -1, GROUP + 2, HEAD_DIM)
    query = rotate(blocks[:, :, :GROUP], pos).astype(jnp.bfloat16)
    key_part = rotate(blocks[:, :, GROUP], pos).astype(jnp.bfloat16)
    value_part = blocks[:, :, GROUP + 1].astype(jnp.bfloat16)
    scores = jnp.einsum(
        "qghd,kgd->ghqk", query, key_part, preferred_element_type=jnp.float32
    ) / math.sqrt(HEAD_DIM)
    same = tenant[:, None] == tenant[None, :]
    causal = pos[None, :] <= pos[:, None]
    near = jnp.logical_or(pos[:, None] - pos[None, :] < WINDOW, pos[None, :] < SINKS)
    allowed = jnp.logical_and(jnp.logical_and(same, causal), near)
    scores = jnp.where(allowed[None, None], scores, -1e30)
    peak = jnp.max(scores, axis=-1, keepdims=True)
    expo = jnp.where(allowed[None, None], jnp.exp(scores - peak), 0.0)
    weights = (expo / jnp.sum(expo, axis=-1, keepdims=True)).astype(jnp.bfloat16)
    mixed = jnp.einsum("ghqk,kgd->qghd", weights, value_part, preferred_element_type=jnp.float32)
    return mixed.reshape(count, -1).astype(jnp.bfloat16)


def shards(tokens, norm_gain, qkv_weight, qkv_bias, lengths):
    tp_count = lax.axis_size("tp")
    req_count = lax.axis_size("req")
    tp_place = lax.axis_index("tp")
    gain_full, bias_full = (
        lax.all_gather(norm_gain.astype(jnp.bfloat16), ("req", "tp"), axis=0, tiled=True),
        lax.all_gather(qkv_bias.astype(jnp.bfloat16), ("req", "tp"), axis=0, tiled=True),
    )
    width = bias_full.shape[0] // tp_count
    bias_block = lax.dynamic_slice_in_dim(bias_full, tp_place * width, width).astype(jnp.float32)
    normed = normalize(tokens, gain_full)
    weight_b = qkv_weight.astype(jnp.bfloat16)
    count = tokens.shape[0]
    gathered = lax.all_gather(weight_b, "req", axis=0, tiled=True)
    regrouped = lax.all_to_all(gathered, "tp", split_axis=1, concat_axis=0, tiled=True)
    shard_rows = weight_b.shape[0]
    reordered = (
        normed.reshape(count, req_count, tp_count, shard_rows)
        .transpose(0, 2, 1, 3)
        .reshape(count, -1)
    )
    joined = jnp.dot(reordered, regrouped, preferred_element_type=jnp.float32)
    joined = joined + bias_block[None, :]
    tenant, pos = positions(lengths[0], count)
    return attend(joined, tenant, pos)


def solution(mesh):
    placed = (
        P("req", None),
        P(("req", "tp")),
        P(("req", "tp"), None),
        P(("req", "tp")),
        P("req", None),
    )
    return jax.shard_map(
        shards, mesh=mesh, in_specs=placed, out_specs=P("req", "tp"), check_vma=False
    )
```

profile of v0, /device:TPU:0, one launch (start us, length us, event | category | flops | bytes accessed | tf_op | source)
XLA Modules:
  0.0 330.9 jit_solution(9403856503985649453)
XLA Ops:
  6.5 0.0 all-gather.2.cloned.1.call-start
  6.5 2.7 convert_element_type.70
  9.3 0.0 all-gather.2.cloned.1.call-update
  9.3 126.2 %all-gather.2.cloned.1.call-done = bf16[896,4608]{1,0:T(8,128)(2,1)} async-done(((bf16[112,4608]{1,0:T(8,128)(2,1)}), bf16[896,4608]{1,0:T(8,128)(2,1)}) %all-gather.2.cloned.1.call-update) | async-done | bytes 8257552 | tf_op jit(solution)/shard_map/all_gather | solution.py:75
  135.5 11.4 %copy.40 = bf16[896,4608]{0,1:T(8,128)(2,1)} copy(bf16[896,4608]{1,0:T(8,128)(2,1)} %all-gather.2.cloned.1.call-done) | data formatting | bytes 16515072 | tf_op jit(solution)/shard_map/all_gather | solution.py:75
  146.9 5.8 %all-to-all-start = ((bf16[896,4,1152]{0,2,1:T(8,128)(2,1)}), bf16[896,4,1152]{0,2,1:T(8,128)(2,1)}, u32[]{:S(2)}, u32[]{:S(2)}) async-start(bf16[896,4,1152]{0,2,1:T(8,128)(2,1)} %bitcast.65), calls=%async_computation | async-start | bytes 16515072 | tf_op jit(solution)/shard_map/all_to_all | solution.py:76
  152.7 0.0 copy-done.2
  152.7 0.0 copy-done.1
  152.7 0.0 copy-done
  152.7 0.2 reduce-window.8
  152.9 0.2 dynamic-update-slice
  153.1 0.2 dynamic-update-slice.1
  153.3 122.7 %all-reduce.2 = (bf16[3584]{0:T(1024)(128)(2,1)S(1)}, bf16[4608]{0:T(1024)(128)(2,1)S(1)}) all-reduce(bf16[3584]{0:T(1024)(128)(2,1)S(1)} %dynamic-update-slice, bf16[4608]{0:T(1024)(128)(2,1)S(1)} %dynamic-update-slice.1), channel_id=1, replica_groups=mesh['req'=8,'tp'=4] {'req','tp'}, use_global_device_ids=true, to_apply=%add | all-reduce | flops 8192 | bytes 32768
  276.0 5.9 %copy.38 = bf16[512,3584]{0,1:T(8,128)(2,1)} copy(bf16[512,3584]{1,0:T(8,128)(2,1)} %param.5) | data formatting | bytes 7340032 | tf_op args[0]
  282.0 2.9 fusion
  284.9 3.1 fusion.2
  288.0 2.0 copy.39
  290.0 0.1 dynamic-slice_convert_fusion
  290.1 0.1 convert_reduce_fusion
  290.2 0.5 fusion.27
  290.7 0.1 pad_maximum_fusion
  290.8 0.5 multiply_cosine_fusion.1
  291.3 0.4 fusion.14
  291.8 0.0 all-to-all-done
  291.8 11.5 %copy.41 = bf16[4,896,1152]{2,1,0:T(8,128)(2,1)} copy(bf16[4,896,1152]{1,2,0:T(8,128)(2,1)} %bitcast.4) | data formatting | bytes 16515072 | tf_op jit(solution)/shard_map/all_to_all | solution.py:76
  303.3 10.8 %convolution_add_fusion = f32[512,1152]{1,0:T(8,128)} fusion(bf16[512,3584]{0,1:T(8,128)(2,1)} %bitcast.72, bf16[3584,1152]{1,0:T(8,128)(2,1)} %bitcast.71, f32[1152]{0:T(1024)S(1)} %dynamic-slice_convert_fusion), kind=kOutput, calls=%fused_computation.13 | convolution fusion | flops 4228448256 | bytes 14291456 | tf_op jit(solution)/shard_map/dot_general | solution.py:83
  314.1 2.2 copy.42
  316.4 0.2 slice_negate_fusion
  316.6 1.7 fusion.3
  318.3 1.8 fusion.4
  320.1 2.7 fusion.10
  322.7 1.3 copy.46
  (14 shorter events, 0.1 us)
Async XLA Ops:
  6.5 128.9 %all-gather.2.cloned.1.call-start = ((), (), s32[]{:S(2)}) async-start(), calls=%async_computation.1 | async-start | bytes 9289728 | tf_op jit(solution)/shard_map/all_gather | solution.py:75
  146.9 5.8 %copy-start.2 = (f32[112]{0:T(128)S(1)}, f32[112]{0:T(128)}, u32[]{:S(2)}) copy-start(f32[112]{0:T(128)} %param.6) | copy-start | bytes 1348
  146.9 5.8 %copy-start.1 = (f32[144]{0:T(256)S(1)}, f32[144]{0:T(256)}, u32[]{:S(2)}) copy-start(f32[144]{0:T(256)} %param.8) | copy-start | bytes 1732
  146.9 5.8 %copy-start = (s32[1,4]{1,0:T(1,128)S(1)}, s32[1,4]{1,0:T(1,128)}, u32[]{:S(2)}) copy-start(s32[1,4]{1,0:T(1,128)} %param.9) | copy-start | bytes 52
  146.9 144.8 %all-to-all-start = ((bf16[896,4,1152]{0,2,1:T(8,128)(2,1)}), bf16[896,4,1152]{0,2,1:T(8,128)(2,1)}, u32[]{:S(2)}, u32[]{:S(2)}) async-start(bf16[896,4,1152]{0,2,1:T(8,128)(2,1)} %bitcast.65), calls=%async_computation | async-start | bytes 16515072 | tf_op jit(solution)/shard_map/all_to_all | solution.py:76
Sparse Core Ops, SparseCore 0:
  9.5 125.8 all-gather.1
where the time goes:
time: 332 us; the launch traced here: 331 us
  waiting for transfers between devices  126 us (38%)
  blocking collectives  123 us (37%)
  local copies, waits for them, and re-layouts  34.9 us (11%)
  matrix products  15.2 us (5%)
  between operations  13.6 us (4%)
  other arithmetic  12.6 us (4%)
  starting transfers between devices  5.76 us (2%)
    all_gather x1, waiting for transfers between devices, shards(): gathered = lax.all_gather(weight_b, 'req', axis=0, tiled=True)  126 us
    unnamed x1, blocking collectives  123 us
    all_to_all x1, local copies, waits for them, and re-layouts, shards(): lax.all_to_all(gathered, 'tp', split_axis=1, concat_axis=0, tiled=True)  11.5 us
    all_gather x1, local copies, waits for them, and re-layouts, shards(): gathered = lax.all_gather(weight_b, 'req', axis=0, tiled=True)  11.4 us
    dot_general x1, matrix products, shards(): joined = jnp.dot(reordered, regrouped, preferred_element_type=jnp.float32)  10.8 us
  transfers between devices with their start and end apart: 2, of which 1 were waited for; matrix products, arithmetic and copies ran while one was open for 5% of the time, Pallas kernels for 0%

commit v1 on v0

--- a/solution.py
+++ b/solution.py
@@ -8,6 +8,15 @@
 SINKS = 4
 GROUP = 7
 WINDOW = 160
+
+
+def copies_detail(page, on_dim):
+    page = jnp.moveaxis(page, 0, on_dim)
+    piece_out = page.shape
+    a_now = page.reshape(
+        *piece_out[:on_dim], piece_out[on_dim] * piece_out[on_dim + 1], *piece_out[on_dim + 2 :]
+    )
+    return a_now
 
 
 def normalize(values, gain):
@@ -72,7 +81,31 @@
     normed = normalize(tokens, gain_full)
     weight_b = qkv_weight.astype(jnp.bfloat16)
     count = tokens.shape[0]
-    gathered = lax.all_gather(weight_b, "req", axis=0, tiled=True)
+
+    def view_compute(q_in, mesh_ax, array_axis):
+        axis_n = lax.axis_size(mesh_ax)
+        inbox = []
+        for k0 in range(axis_n):
+            inbox.append((k0, (k0 + 1) % axis_n))
+        slots = []
+        for rr, pp in inbox:
+            slots.append((pp, rr))
+        carry, x_now = ([], [])
+        for h in range(axis_n - 1):
+            if h % 2 == 0:
+                carry.append(
+                    lax.ppermute(carry[-1] if carry else q_in, axis_name=mesh_ax, perm=inbox)
+                )
+            else:
+                x_now.append(lax.ppermute(x_now[-1] if x_now else q_in, mesh_ax, slots))
+        block_now = jnp.stack([*carry[::-1], q_in, *x_now], 0)
+        z1 = lax.axis_index(mesh_ax)
+        current_value = z1 - len(carry)
+        block_now = block_now[(jnp.arange(axis_n) - current_value) % axis_n]
+        new = copies_detail(block_now, array_axis)
+        return new
+
+    gathered = view_compute(weight_b, "req", 0)
     regrouped = lax.all_to_all(gathered, "tp", split_axis=1, concat_axis=0, tiled=True)
     shard_rows = weight_b.shape[0]
     reordered = (

time: 332 us -> 376 us (1.13)
  starting transfers between devices: 5.76 us -> 66.3 us
  waiting for transfers between devices: 126 us -> 103 us
  local copies, waits for them, and re-layouts: 34.9 us -> 52.7 us
  between operations: 13.6 us -> 0.21 us
    all_gather x1 -> x0, waiting for transfers between devices: 126 us -> none  [shards(): gathered = lax.all_gather(weight_b, 'req', axis=0, tiled=True)]
    ppermute x0 -> x7, waiting for transfers between devices: none -> 103 us  [the longest x4 103 us: view_compute(): lax.ppermute(carry[-1] if carry else q_in, axis_name=mesh_ax, perm=inbox)]
    ppermute x0 -> x7, starting transfers between devices: none -> 60.5 us  [the longest x3 52.4 us: view_compute(): x_now.append(lax.ppermute(x_now[-1] if x_now else q_in, mesh_ax, slots))]
    unnamed x11 -> x21, local copies, waits for them, and re-layouts: 6.38 us -> 18.9 us
    all_gather x1 -> x0, local copies, waits for them, and re-layouts: 11.4 us -> none  [shards(): gathered = lax.all_gather(weight_b, 'req', axis=0, tiled=True)]
    gather x0 -> x1, local copies, waits for them, and re-layouts: none -> 7.97 us  [view_compute(): block_now = block_now[(jnp.arange(axis_n) - current_value) % axis_n]]
    all_to_all x1 -> x2, local copies, waits for them, and re-layouts: 11.5 us -> 19.2 us  [shards(): lax.all_to_all(gathered, 'tp', split_axis=1, concat_axis=0, tiled=True)]
  transfers between devices with their start and end apart: 2 -> 8, of which waited for: 1 -> 4; matrix products, arithmetic and copies ran while one was open for 5% -> 8% of each run, Pallas kernels for 0% -> 0%
where the time goes in v1:
time: 376 us; the launch traced here: 375 us
  blocking collectives  125 us (33%)
  waiting for transfers between devices  103 us (27%)
  starting transfers between devices  66.3 us (18%)
  local copies, waits for them, and re-layouts  52.7 us (14%)
  matrix products  15.2 us (4%)
  other arithmetic  12.8 us (3%)
    unnamed x1, blocking collectives  125 us
    ppermute x4, waiting for transfers between devices, view_compute(): lax.ppermute(carry[-1] if carry else q_in, axis_name=mesh_ax, perm=inbox)  103 us
    ppermute x3, starting transfers between devices, view_compute(): x_now.append(lax.ppermute(x_now[-1] if x_now else q_in, mesh_ax, slots))  52.4 us
    all_to_all x2, local copies, waits for them, and re-layouts, shards(): lax.all_to_all(gathered, 'tp', split_axis=1, concat_axis=0, tiled=True)  19.2 us
    unnamed x21, local copies, waits for them, and re-layouts  18.9 us
    dot_general x1, matrix products, shards(): joined = jnp.dot(reordered, regrouped, preferred_element_type=jnp.float32)  10.9 us
    ppermute x4, starting transfers between devices, view_compute(): lax.ppermute(carry[-1] if carry else q_in, axis_name=mesh_ax, perm=inbox)  8.06 us
    gather x1, local copies, waits for them, and re-layouts, view_compute(): block_now = block_now[(jnp.arange(axis_n) - current_value) % axis_n]  7.97 us
  transfers between devices with their start and end apart: 8, of which 4 were waited for; matrix products, arithmetic and copies ran while one was open for 8% of the time, Pallas kernels for 0%

profile of v1, /device:TPU:0, one launch (start us, length us, event | category | flops | bytes accessed | tf_op | source)
XLA Modules:
  0.0 374.9 jit_solution(3140960782152446073)
XLA Ops:
  0.0 1.8 convert_element_type.70
  1.8 3.0 collective-permute-start
  4.8 25.8 %collective-permute-done = bf16[112,4608]{1,0:T(8,128)(2,1)S(1)} collective-permute-done((bf16[112,4608]{1,0:T(8,128)(2,1)S(1)}, bf16[112,4608]{1,0:T(8,128)(2,1)S(1)}, u32[]{:S(2)}, u32[]{:S(2)}) %collective-permute-start) | collective-permute-done | bytes 1032224 | tf_op jit(solution)/shard_map/ppermute | solution.py:97
  30.7 4.7 %collective-permute-start.4 = (bf16[112,4608]{1,0:T(8,128)(2,1)S(1)}, bf16[112,4608]{1,0:T(8,128)(2,1)}, u32[]{:S(2)}, u32[]{:S(2)}) collective-permute-start(bf16[112,4608]{1,0:T(8,128)(2,1)S(1)} %convert_element_type.70), channel_id=1, source_target_pairs={{4,0},{8,4},{12,8},{16,12},{20,16},{24,20},{28,24},{0,28},{5,1},{9... | collective-permute-start | bytes 3096584 | tf_op jit(solution)/shard_map/ppermute | solution.py:100
  35.4 39.2 %collective-permute-done.1 = bf16[112,4608]{1,0:T(8,128)(2,1)S(1)} collective-permute-done((bf16[112,4608]{1,0:T(8,128)(2,1)S(1)}, bf16[112,4608]{1,0:T(8,128)(2,1)S(1)}, u32[]{:S(2)}, u32[]{:S(2)}) %collective-permute-start.1) | collective-permute-done | bytes 1032224 | tf_op jit(solution)/shard_map/ppermute | solution.py:97
  74.6 2.5 collective-permute-start.2
  77.1 23.1 %collective-permute-start.5 = (bf16[112,4608]{1,0:T(8,128)(2,1)}, bf16[112,4608]{1,0:T(8,128)(2,1)}, u32[]{:S(2)}, u32[]{:S(2)}) collective-permute-start(bf16[112,4608]{1,0:T(8,128)(2,1)} %collective-permute-done.4), channel_id=1, source_target_pairs={{4,0},{8,4},{12,8},{16,12},{20,16},{24,20},{28,24},{0,28},{5,1},{9... | collective-permute-start | bytes 3096584 | tf_op jit(solution)/shard_map/ppermute | solution.py:100
  100.2 20.0 %collective-permute-done.2 = bf16[112,4608]{1,0:T(8,128)(2,1)} collective-permute-done((bf16[112,4608]{1,0:T(8,128)(2,1)S(1)}, bf16[112,4608]{1,0:T(8,128)(2,1)}, u32[]{:S(2)}, u32[]{:S(2)}) %collective-permute-start.2) | collective-permute-done | bytes 1032224 | tf_op jit(solution)/shard_map/ppermute | solution.py:97
  120.2 2.6 collective-permute-start.3
  122.8 24.6 %collective-permute-start.6 = (bf16[112,4608]{1,0:T(8,128)(2,1)}, bf16[112,4608]{1,0:T(8,128)(2,1)S(1)}, u32[]{:S(2)}, u32[]{:S(2)}) collective-permute-start(bf16[112,4608]{1,0:T(8,128)(2,1)} %collective-permute-done.5), channel_id=1, source_target_pairs={{4,0},{8,4},{12,8},{16,12},{20,16},{24,20},{28,24},{0,28},{5,1},{9... | collective-permute-start | bytes 3096584 | tf_op jit(solution)/shard_map/ppermute | solution.py:100
  147.5 17.9 %collective-permute-done.3 = bf16[112,4608]{1,0:T(8,128)(2,1)} collective-permute-done((bf16[112,4608]{1,0:T(8,128)(2,1)}, bf16[112,4608]{1,0:T(8,128)(2,1)}, u32[]{:S(2)}, u32[]{:S(2)}) %collective-permute-start.3) | collective-permute-done | bytes 1032224 | tf_op jit(solution)/shard_map/ppermute | solution.py:97
  165.4 2.3 bitcast_dynamic-update-slice_fusion.7
  167.6 2.3 bitcast_dynamic-update-slice_fusion.6
  169.9 2.3 bitcast_dynamic-update-slice_fusion.5
  173.2 1.1 bitcast_dynamic-update-slice_fusion.3
  174.3 2.3 bitcast_dynamic-update-slice_fusion.2
  176.6 2.3 bitcast_dynamic-update-slice_fusion.1
  179.9 8.0 %gather_fusion = bf16[8,112,4608]{2,1,0:T(8,128)(2,1)} fusion(bf16[8,112,4608]{2,1,0:T(8,128)(2,1)} %bitcast_dynamic-update-slice_fusion, s32[1024]{0:T(1024)S(1)} %pad_clamp_fusion), kind=kCustom, calls=%fused_computation | custom fusion | bytes 16515104 | tf_op jit(solution)/shard_map/gather | solution.py:104
  187.9 11.7 %all_to_all.14 = bf16[896,4,1152]{2,1,0:T(4,128)(2,1)} reshape(bf16[8,112,4608]{2,1,0:T(8,128)(2,1)} %gather_fusion) | data formatting | bytes 16515072 | tf_op jit(solution)/shard_map/all_to_all | solution.py:109
  199.5 7.6 %copy.38 = bf16[896,4,1152]{2,0,1:T(8,128)(2,1)} copy(bf16[896,4,1152]{2,1,0:T(4,128)(2,1)} %all_to_all.14) | data formatting | bytes 16515072 | tf_op jit(solution)/shard_map/all_to_all | solution.py:109
  207.1 5.8 %all-to-all-start = ((bf16[896,4,1152]{2,0,1:T(8,128)(2,1)}), bf16[896,4,1152]{2,0,1:T(8,128)(2,1)}, u32[]{:S(2)}, u32[]{:S(2)}) async-start(bf16[896,4,1152]{2,0,1:T(8,128)(2,1)} %copy.38), calls=%async_computation | async-start | bytes 16515072 | tf_op jit(solution)/shard_map/all_to_all | solution.py:109
  213.4 124.7 %all-reduce.2 = (bf16[3584]{0:T(1024)(128)(2,1)S(1)}, bf16[4608]{0:T(1024)(128)(2,1)S(1)}) all-reduce(bf16[3584]{0:T(1024)(128)(2,1)S(1)} %dynamic-update-slice, bf16[4608]{0:T(1024)(128)(2,1)S(1)} %dynamic-update-slice.1), channel_id=1, replica_groups=mesh['req'=8,'tp'=4] {'req','tp'}, use_global_device_ids=true, to_apply=%add | all-reduce | flops 8192 | bytes 32768
  338.1 6.0 %copy.36 = bf16[512,3584]{0,1:T(8,128)(2,1)} copy(bf16[512,3584]{1,0:T(8,128)(2,1)} %param.5) | data formatting | bytes 7340032 | tf_op args[0]
  344.1 2.9 fusion
  347.0 3.1 fusion.2
  350.1 2.0 copy.37
  354.1 10.9 %convolution_add_fusion = f32[512,1152]{1,0:T(8,128)} fusion(bf16[512,3584]{0,1:T(8,128)(2,1)} %bitcast.88, bf16[3584,1152]{1,0:T(8,128)(2,1)} %bitcast.13, f32[1152]{0:T(1024)S(1)} %dynamic-slice_convert_fusion), kind=kOutput, calls=%fused_computation.14 | convolution fusion | flops 4228448256 | bytes 14291456 | tf_op jit(solution)/shard_map/dot_general | solution.py:116
  365.0 2.3 copy.39
  367.5 1.6 fusion.3
  369.1 1.8 fusion.4
  370.9 2.7 fusion.10
  373.6 1.3 copy.43
  (40 shorter events, 4.7 us)
Async XLA Ops:
  0.0 173.2 %copy-start = (f32[112,4608]{1,0:T(8,128)S(1)}, f32[112,4608]{1,0:T(8,128)}, u32[]{:S(2)}) copy-start(f32[112,4608]{1,0:T(8,128)} %param.7) | copy-start | bytes 6193156
  1.8 28.8 %collective-permute-start = (bf16[112,4608]{1,0:T(8,128)(2,1)S(1)}, bf16[112,4608]{1,0:T(8,128)(2,1)S(1)}, u32[]{:S(2)}, u32[]{:S(2)}) collective-permute-start(bf16[112,4608]{1,0:T(8,128)(2,1)S(1)} %convert_element_type.70), channel_id=1, source_target_pairs={{0,4},{4,8},{8,12},{12,16},{16,20},{20,24},{24,28},{28,0},{1,5},{5... | collective-permute-start | bytes 3096584 | tf_op jit(solution)/shard_map/ppermute | solution.py:97
  30.7 43.9 %collective-permute-start.1 = (bf16[112,4608]{1,0:T(8,128)(2,1)S(1)}, bf16[112,4608]{1,0:T(8,128)(2,1)S(1)}, u32[]{:S(2)}, u32[]{:S(2)}) collective-permute-start(bf16[112,4608]{1,0:T(8,128)(2,1)S(1)} %collective-permute-done), channel_id=1, source_target_pairs={{0,4},{4,8},{8,12},{12,16},{16,20},{20,24},{24,28},{28,0},{1,5},{5... | collective-permute-start | bytes 3096584 | tf_op jit(solution)/shard_map/ppermute | solution.py:97
  30.7 46.4 %collective-permute-start.4 = (bf16[112,4608]{1,0:T(8,128)(2,1)S(1)}, bf16[112,4608]{1,0:T(8,128)(2,1)}, u32[]{:S(2)}, u32[]{:S(2)}) collective-permute-start(bf16[112,4608]{1,0:T(8,128)(2,1)S(1)} %convert_element_type.70), channel_id=1, source_target_pairs={{4,0},{8,4},{12,8},{16,12},{20,16},{24,20},{28,24},{0,28},{5,1},{9... | collective-permute-start | bytes 3096584 | tf_op jit(solution)/shard_map/ppermute | solution.py:100
  74.6 2.5 copy-start.1
  74.6 45.6 %collective-permute-start.2 = (bf16[112,4608]{1,0:T(8,128)(2,1)S(1)}, bf16[112,4608]{1,0:T(8,128)(2,1)}, u32[]{:S(2)}, u32[]{:S(2)}) collective-permute-start(bf16[112,4608]{1,0:T(8,128)(2,1)S(1)} %collective-permute-done.1), channel_id=1, source_target_pairs={{0,4},{4,8},{8,12},{12,16},{16,20},{20,24},{24,28},{28,0},{1,5},{5... | collective-permute-start | bytes 3096584 | tf_op jit(solution)/shard_map/ppermute | solution.py:97
  77.1 45.8 %collective-permute-start.5 = (bf16[112,4608]{1,0:T(8,128)(2,1)}, bf16[112,4608]{1,0:T(8,128)(2,1)}, u32[]{:S(2)}, u32[]{:S(2)}) collective-permute-start(bf16[112,4608]{1,0:T(8,128)(2,1)} %collective-permute-done.4), channel_id=1, source_target_pairs={{4,0},{8,4},{12,8},{16,12},{20,16},{24,20},{28,24},{0,28},{5,1},{9... | collective-permute-start | bytes 3096584 | tf_op jit(solution)/shard_map/ppermute | solution.py:100
  120.2 45.1 %collective-permute-start.3 = (bf16[112,4608]{1,0:T(8,128)(2,1)}, bf16[112,4608]{1,0:T(8,128)(2,1)}, u32[]{:S(2)}, u32[]{:S(2)}) collective-permute-start(bf16[112,4608]{1,0:T(8,128)(2,1)} %collective-permute-done.2), channel_id=1, source_target_pairs={{0,4},{4,8},{8,12},{12,16},{16,20},{20,24},{24,28},{28,0},{1,5},{5... | collective-permute-start | bytes 3096584 | tf_op jit(solution)/shard_map/ppermute | solution.py:97
  122.8 56.0 %collective-permute-start.6 = (bf16[112,4608]{1,0:T(8,128)(2,1)}, bf16[112,4608]{1,0:T(8,128)(2,1)S(1)}, u32[]{:S(2)}, u32[]{:S(2)}) collective-permute-start(bf16[112,4608]{1,0:T(8,128)(2,1)} %collective-permute-done.5), channel_id=1, source_target_pairs={{4,0},{8,4},{12,8},{16,12},{20,16},{24,20},{28,24},{0,28},{5,1},{9... | collective-permute-start | bytes 3096584 | tf_op jit(solution)/shard_map/ppermute | solution.py:100
  207.1 5.8 %copy-start.3 = (f32[144]{0:T(256)S(1)}, f32[144]{0:T(256)}, u32[]{:S(2)}) copy-start(f32[144]{0:T(256)} %param.8) | copy-start | bytes 1732
  207.1 5.8 %copy-start.4 = (f32[112]{0:T(128)S(1)}, f32[112]{0:T(128)}, u32[]{:S(2)}) copy-start(f32[112]{0:T(128)} %param.6) | copy-start | bytes 1348
  207.1 147.0 %all-to-all-start = ((bf16[896,4,1152]{2,0,1:T(8,128)(2,1)}), bf16[896,4,1152]{2,0,1:T(8,128)(2,1)}, u32[]{:S(2)}, u32[]{:S(2)}) async-start(bf16[896,4,1152]{2,0,1:T(8,128)(2,1)} %copy.38), calls=%async_computation | async-start | bytes 16515072 | tf_op jit(solution)/shard_map/all_to_all | solution.py:109
  347.0 5.2 %copy-start.2 = (s32[1,4]{1,0:T(1,128)S(1)}, s32[1,4]{1,0:T(1,128)}, u32[]{:S(2)}) copy-start(s32[1,4]{1,0:T(1,128)} %param.9) | copy-start | bytes 52
